TPU v7x, 32 devices: a whole 2x2x4 slice. The times are simulated.
32 devices in a mesh: eta: 2 (over x), phi: 4 (over z), replica: 4 (over y, core).
Axes of the slice: x: 2, y: 2, z: 4, core: 2. Of those that a mesh axis runs over, the one named last changes fastest.
Arguments:
- tokens: bfloat16 [4, 64, 128, 768], P('replica', 'eta', 'phi'), may hold values from -6 to 6
- send_pos: int32 [4, 2, 4, 8, 35], P('replica', 'eta', 'phi'), may hold values from 0 to 1024, as said below
- enc_src: int32 [4, 2, 4, 256], P('replica', 'eta', 'phi'), may hold values from 0 to 279, as said below
- window_id: int32 [4, 2, 4, 256], P('replica', 'eta', 'phi'), may hold values from 0 to 3
- enc_cot: bfloat16 [4, 2, 4, 256, 768], P('replica', 'eta', 'phi'), may hold values from -0.0625 to 0.0625
- w_qkv: bfloat16 [768, 2304], replicated, may hold values from -0.21875 to 0.21875
- head_scale: float32 [12], replicated, may hold values from 2 to 12
- w_out: bfloat16 [768, 768], replicated, may hold values from -0.21875 to 0.21875
- w_dec_in: bfloat16 [768, 384], replicated, may hold values from -0.21875 to 0.21875
- mask_token: bfloat16 [384], replicated, may hold values from -4 to 4
- conv_kernel: float32 [7, 7, 384], replicated, may hold values from -0.875 to 0.875
- w_up: bfloat16 [384, 768], replicated, may hold values from -0.3125 to 0.3125
- w_down: bfloat16 [768, 384], replicated, may hold values from -0.21875 to 0.21875
- w_head: bfloat16 [384, 128], replicated, may hold values from -0.3125 to 0.3125
Outputs:
- weight_grads: float32 [3072, 768], P(('eta', 'phi'))
- reconstruction: float32 [4, 64, 128, 128], P('replica', 'eta', 'phi')
Inputs may be any that keep to these rules, and one draw needn't show every extreme that they name: send_pos[e,a,b,d,k] is the cell of the k-th visible token that tile (a,b) sends to encoder shard d; 1024 marks an empty slot and empty slots follow the live ones. The visible cells of a tile are whole aligned 2 x 2 blocks, each sent exactly once; every encoder shard receives exactly 256 live slots; some tile fills all 35 slots to some shard. enc_src[e,a,b,r] = s * 35 + k names a live slot (send_pos of tile s towards this shard, slot k); each live slot arriving at the shard appears exactly once.
All inputs are finite; a program needn't handle non-finite values.
Results may differ from a plain program's by a relative error of at most 0.0095.
Values may be sent and summed in bfloat16 or wider, within the bound.
No kernel may reach another device: no remote copies, remote signals or barrier semaphores. Data moves between devices by JAX's collectives and lax.ppermute only.
A program may use at most 128 MiB of HBM per device.

v0:
```python
import jax
import jax.numpy as jnp
from jax import lax
from jax.sharding import PartitionSpec as P

norm_eps = 1e-05
length_eps = 1e-06
highest = lax.Precision.HIGHEST


def extended(block, sides, width):
    for axis, dim in sides:
        count = lax.axis_size(axis)
        forward = [(i, i + 1) for i in range(count - 1)]
        forward.append((count - 1, 0))
        backward = [(target, source) for source, target in forward]
        low = lax.ppermute(
            lax.slice_in_dim(block, block.shape[dim] - width, None, axis=dim), axis, forward
        )
        high = lax.ppermute(lax.slice_in_dim(block, 0, width, axis=dim), axis, backward)
        block = jnp.concatenate([low, block, high], axis=dim)
    return block


def plain_norm(values):
    centre = jnp.mean(values, axis=-1, keepdims=True)
    centred = values - centre
    spread = jnp.mean(centred * centred, axis=-1, keepdims=True)
    return centred * lax.rsqrt(spread + norm_eps)


def encoder_pass(enc_in, window, cotangent, w_qkv, head_scale, w_out):
    row_count, feature_width = enc_in.shape
    head_count = head_scale.shape[0]
    head_size = feature_width // head_count
    normed = plain_norm(enc_in.astype(jnp.float32)).astype(jnp.bfloat16)
    qkv = jnp.dot(normed, w_qkv, preferred_element_type=jnp.float32).reshape(
        row_count, 3, head_count, head_size
    )
    query = qkv[:, 0]
    keyed = qkv[:, 1]
    value_low = qkv[:, 2].astype(jnp.bfloat16)
    query_len = jnp.sqrt(jnp.sum(query * query, axis=-1, keepdims=True) + length_eps)
    key_len = jnp.sqrt(jnp.sum(keyed * keyed, axis=-1, keepdims=True) + length_eps)
    query_unit = query / query_len
    key_unit = keyed / key_len
    same_window = window[:, None] == window[None, :]
    scores = (
        jnp.einsum("qhd,khd->hqk", query_unit, key_unit, precision=highest)
        * head_scale[:, None, None]
    )
    raised = jnp.where(same_window[None], jnp.exp(scores), jnp.zeros((), jnp.float32))
    softmax_weights = raised / jnp.sum(raised, axis=-1, keepdims=True)
    softmax_low = softmax_weights.astype(jnp.bfloat16)
    attended = jnp.einsum(
        "hqk,khd->qhd", softmax_low, value_low, preferred_element_type=jnp.float32
    )
    attended = attended.reshape(row_count, feature_width).astype(jnp.bfloat16)
    enc_out = (
        enc_in.astype(jnp.float32) + jnp.dot(attended, w_out, preferred_element_type=jnp.float32)
    ).astype(jnp.bfloat16)
    grad_attended = lax.dot_general(
        cotangent, w_out, (((1,), (1,)), ((), ())), preferred_element_type=jnp.float32
    )
    grad_attended = grad_attended.astype(jnp.bfloat16).reshape(row_count, head_count, head_size)
    grad_soft = jnp.einsum(
        "qhd,khd->hqk", grad_attended, value_low, preferred_element_type=jnp.float32
    )
    grad_value = jnp.einsum(
        "hqk,qhd->khd", softmax_low, grad_attended, preferred_element_type=jnp.float32
    )
    grad_scores = softmax_weights * (
        grad_soft - jnp.sum(softmax_weights * grad_soft, axis=-1, keepdims=True)
    )
    grad_scores = grad_scores * head_scale[:, None, None]
    grad_qunit = jnp.einsum("hqk,khd->qhd", grad_scores, key_unit, precision=highest)
    grad_kunit = jnp.einsum("hqk,qhd->khd", grad_scores, query_unit, precision=highest)
    grad_query = (
        grad_qunit - query_unit * jnp.sum(query_unit * grad_qunit, axis=-1, keepdims=True)
    ) / query_len
    grad_key = (
        grad_kunit - key_unit * jnp.sum(key_unit * grad_kunit, axis=-1, keepdims=True)
    ) / key_len
    grad_qkv = (
        jnp.stack([grad_query, grad_key, grad_value], axis=1)
        .reshape(row_count, 3 * feature_width)
        .astype(jnp.bfloat16)
    )
    contract_rows = (((0,), (0,)), ((), ()))
    term = jnp.concatenate(
        [
            lax.dot_general(grad_qkv, normed, contract_rows, preferred_element_type=jnp.float32),
            lax.dot_general(cotangent, attended, contract_rows, preferred_element_type=jnp.float32),
        ],
        axis=0,
    )
    return (enc_out, term)


def body(
    tokens,
    send_pos,
    enc_src,
    window_id,
    enc_cot,
    w_qkv,
    head_scale,
    w_out,
    w_dec_in,
    mask_token,
    conv_kernel,
    w_up,
    w_down,
    w_head,
):
    eta_cells = tokens.shape[1]
    phi_cells = tokens.shape[2]
    feature_width = tokens.shape[3]
    dec_width = w_dec_in.shape[1]
    tile_len = eta_cells * phi_cells
    eta_count = lax.axis_size("eta")
    phi_count = lax.axis_size("phi")
    group_size = eta_count * phi_count
    slot_count = send_pos.shape[-1]
    flat_tile = tokens.reshape(tile_len, feature_width)
    slot_cells = send_pos.reshape(group_size * slot_count)
    outgoing = jnp.take(flat_tile, jnp.minimum(slot_cells, tile_len - 1), axis=0)
    outgoing = outgoing.reshape(group_size, slot_count, feature_width)
    arrived = lax.all_to_all(outgoing, ("eta", "phi"), split_axis=0, concat_axis=0, tiled=True)
    arrived = arrived.reshape(group_size * slot_count, feature_width)
    sources = enc_src.reshape(-1)
    enc_in = jnp.take(arrived, sources, axis=0)
    enc_out, term = encoder_pass(
        enc_in, window_id.reshape(-1), enc_cot.reshape(-1, feature_width), w_qkv, head_scale, w_out
    )
    grad_share = lax.psum_scatter(term, ("eta", "phi", "replica"), scatter_dimension=0, tiled=True)
    grad_total = lax.all_gather(
        grad_share.astype(jnp.bfloat16), "replica", axis=0, tiled=True
    ).astype(grad_share.dtype)
    outbound = (
        jnp.zeros((group_size * slot_count, feature_width), jnp.bfloat16).at[sources].set(enc_out)
    )
    returned = lax.all_to_all(
        outbound.reshape(group_size, slot_count, feature_width),
        ("eta", "phi"),
        split_axis=0,
        concat_axis=0,
        tiled=True,
    )
    returned = returned.reshape(group_size * slot_count, feature_width)
    dec_slots = jnp.dot(returned, w_dec_in, preferred_element_type=jnp.float32).astype(jnp.bfloat16)
    filled = (
        jnp.zeros((tile_len, dec_width), jnp.bfloat16).at[slot_cells].set(dec_slots, mode="drop")
    )
    seen_cells = jnp.zeros((tile_len,), jnp.bool_).at[slot_cells].set(True, mode="drop")
    dec_grid = jnp.where(seen_cells[:, None], filled, mask_token).reshape(
        eta_cells, phi_cells, dec_width
    )
    kernel_span = conv_kernel.shape[0]
    rim_width = kernel_span // 2
    padded = extended(dec_grid, (("eta", 0), ("phi", 1)), rim_width)
    eta_place = lax.axis_index("eta")
    rim_line = lax.broadcasted_iota(jnp.int32, (eta_cells + 2 * rim_width, 1, 1), 0)
    keep_rim = jnp.logical_and(
        jnp.logical_or(rim_line >= rim_width, eta_place > 0),
        jnp.logical_or(rim_line < eta_cells + rim_width, eta_place < eta_count - 1),
    )
    padded = jnp.where(keep_rim, padded, jnp.zeros((), padded.dtype))
    mixed_cells = jnp.zeros((eta_cells, phi_cells, dec_width), jnp.float32)
    for row_shift in range(kernel_span):
        for col_shift in range(kernel_span):
            window_cells = padded[
                row_shift : row_shift + eta_cells, col_shift : col_shift + phi_cells
            ].astype(jnp.float32)
            mixed_cells = mixed_cells + conv_kernel[row_shift, col_shift] * window_cells
    dec_normed = plain_norm(mixed_cells).astype(jnp.bfloat16).reshape(tile_len, dec_width)
    hidden = jax.nn.gelu(
        jnp.dot(dec_normed, w_up, preferred_element_type=jnp.float32), approximate=False
    ).astype(jnp.bfloat16)
    decoded = (
        dec_grid.reshape(tile_len, dec_width).astype(jnp.float32)
        + jnp.dot(hidden, w_down, preferred_element_type=jnp.float32)
    ).astype(jnp.bfloat16)
    reconstruction = jnp.dot(decoded, w_head, preferred_element_type=jnp.float32).reshape(
        1, eta_cells, phi_cells, -1
    )
    return (grad_total, reconstruction)


def solution(mesh):
    in_specs = (
        P("replica", "eta", "phi", None),
        P("replica", "eta", "phi", None, None),
        P("replica", "eta", "phi", None),
        P("replica", "eta", "phi", None),
        P("replica", "eta", "phi", None, None),
        P(),
        P(),
        P(),
        P(),
        P(),
        P(),
        P(),
        P(),
        P(),
    )
    out_specs = (P(("eta", "phi"), None), P("replica", "eta", "phi", None))
    return jax.shard_map(body, mesh=mesh, in_specs=in_specs, out_specs=out_specs, check_vma=False)
```

profile of v0, /device:TPU:0, one launch (start us, length us, event | category | flops | bytes accessed | tf_op | source)
XLA Modules:
  0.0 229.6 jit_solution(4999208129221974570)
XLA Ops:
  7.2 0.8 compare_and_fusion
  8.0 0.9 reshape.238
  9.0 0.6 fusion.50
  9.6 4.6 %gather_fusion = bf16[280,768]{1,0:T(8,128)(2,1)} fusion(bf16[1024,768]{1,0:T(8,128)(2,1)} %bitcast.105, s32[1024]{0:T(1024)S(1)} %pad_clamp_fusion.1), kind=kCustom, calls=%fused_computation | custom fusion | bytes 861280 | tf_op jit(solution)/shard_map/jit(_take)/gather | solution.py:127
  14.1 1.9 gather.11
  16.1 1.9 broadcast_select_fusion.1
  18.0 7.3 %all-to-all-start = ((bf16[8,35,768]{2,1,0:T(8,128)(2,1)}), bf16[8,35,768]{2,1,0:T(8,128)(2,1)}, u32[]{:S(2)}, u32[]{:S(2)}) async-start(bf16[8,35,768]{2,1,0:T(8,128)(2,1)} %broadcast_select_fusion.1), calls=%async_computation | async-start | bytes 983040 | tf_op jit(solution)/shard_map/all_to_all | solution.py:129
  25.3 2.6 %convolution_convert_fusion.2 = bf16[256,768]{1,0:T(8,128)(2,1)} fusion(bf16[768,768]{1,0:T(8,128)(2,1)} %param.21, bf16[1,1,1,256,768]{4,3,2,1,0:T(8,128)(2,1)} %param.18), kind=kOutput, calls=%fused_computation.52 | convolution fusion | flops 302186496 | bytes 1966080 | tf_op jit(solution)/shard_map/dot_general | solution.py:62
  28.0 1.9 copy.32
  29.9 0.7 compare_and_fusion.1
  30.6 0.7 broadcast_compare_fusion
  31.3 8.7 %all-to-all-done = bf16[8,35,768]{2,1,0:T(8,128)(2,1)} async-done(((bf16[8,35,768]{2,1,0:T(8,128)(2,1)}), bf16[8,35,768]{2,1,0:T(8,128)(2,1)}, u32[]{:S(2)}, u32[]{:S(2)}) %all-to-all-start) | async-done | bytes 430112 | tf_op jit(solution)/shard_map/all_to_all | solution.py:129
  40.0 1.9 reshape.239
  42.0 3.2 %gather_fusion.1 = bf16[256,768]{1,0:T(8,128)(2,1)} fusion(bf16[280,768]{1,0:T(8,128)(2,1)} %reshape.239, s32[1024]{0:T(1024)S(1)} %pad_clamp_fusion), kind=kCustom, calls=%fused_computation.1 | custom fusion | bytes 787456 | tf_op jit(solution)/shard_map/jit(_take)/gather | solution.py:132
  45.2 1.2 convert_reduce_fusion
  46.4 1.3 fusion.29
  47.7 2.6 %fusion.53 = f32[256,2304]{0,1:T(8,128)S(1)} fusion(bf16[768,2304]{1,0:T(8,128)(2,1)S(1)} %copy-done, f32[256]{0:T(256)S(1)} %add_rsqrt_fusion.1, f32[256]{0:T(256)S(1)} %broadcast_multiply_fusion.1, bf16[256,768]{1,0:T(8,128)(2,1)} %gather_fusion.1, pred[256]{0:T(512)(128)(4,1)S(1)} %compare_and_fusion.1), kind=kOutput, calls=%fused_computation.163 | convolution fusion | flops 906952704 | bytes 6293760 | tf_op jit(solution)/shard_map/dot_general | solution.py:37
  50.4 0.2 multiply_reduce_fusion.3
  50.6 0.6 copy-done.6
  51.2 3.4 %fusion.13 = (f32[12,256]{1,0:T(8,128)S(1)}, f32[12,256,256]{1,2,0:T(8,128)S(1)}) fusion(f32[12]{0:T(128)S(1)} %copy-done.44, pred[256,256]{0,1:T(8,128)(4,1)S(1)} %copy-done.6, f32[256,3,12,64]{0,3,2,1:T(8,128)S(1)} %bitcast.107, f32[256,12]{0,1:T(8,128)S(1)} %get-tuple-element.66, f32[256,12]{0,1:T(8,128)S(1)} %get-tuple-element.65), kind=kOutput, calls=%fused_computation.31 | convolution fusion | flops 606729216 | bytes 4829696 | tf_op jit(solution)/shard_map/qhd,khd->hqk/dot_general | solution.py:49
  54.6 0.9 convolution_convert_fusion
  55.5 0.1 copy-done.5
  55.6 0.9 fusion.24
  56.4 1.2 multiply_reduce_fusion
  57.6 4.1 %convolution_bitcast_fusion.1 = f32[256,12,64]{0,2,1:T(8,128)S(1)} fusion(f32[12,256,256]{1,2,0:T(8,128)S(1)} %get-tuple-element.64, f32[12,256]{1,0:T(8,128)S(1)} %get-tuple-element.63, f32[12]{0:T(128)S(1)} %copy-done.44, f32[256,3,12,64]{0,3,2,1:T(8,128)S(1)} %bitcast.110, f32[256,12]{0,1:T(8,128)S(1)} %get-tuple-element.65, ...), kind=kOutput, calls=%fused_computation.44 | convolution fusion | flops 608894976 | bytes 7979520 | tf_op jit(solution)/shard_map/hqk,qhd->khd/dot_general | solution.py:77
  61.7 3.1 %convolution_bitcast_fusion.2 = f32[256,12,64]{0,2,1:T(8,128)S(1)} fusion(f32[12,256,256]{1,2,0:T(8,128)S(1)} %get-tuple-element.64, f32[12,256]{1,0:T(8,128)S(1)} %get-tuple-element.63, f32[12]{0:T(128)S(1)} %copy-done.44, f32[256,3,12,64]{0,3,2,1:T(8,128)S(1)} %bitcast.111, f32[256,12]{0,1:T(8,128)S(1)} %get-tuple-element.66, ...), kind=kOutput, calls=%fused_computation.45 | convolution fusion | flops 608894976 | bytes 7979520 | tf_op jit(solution)/shard_map/hqk,khd->qhd/dot_general | solution.py:76
  64.8 1.9 convolution_bitcast_fusion
  66.8 0.2 fusion.25
  67.0 0.2 fusion.26
  67.3 0.1 pad_maximum_fusion.1
  67.4 0.8 copy-done.1
  68.3 4.1 %fusion.51 = f32[2304,768]{1,0:T(8,128)} fusion(bf16[256,2304]{0,1:T(8,128)(2,1)S(1)} %bitcast.104, f32[256]{0:T(256)S(1)} %add_rsqrt_fusion.1, f32[256]{0:T(256)S(1)} %broadcast_multiply_fusion.1, bf16[256,768]{1,0:T(8,128)(2,1)S(1)} %copy-done.1, pred[256]{0:T(512)(128)(4,1)S(1)} %compare_and_fusion.1), kind=kOutput, calls=%fused_computation.162 | convolution fusion | flops 906952704 | bytes 8653056 | tf_op jit(solution)/shard_map/dot_general | solution.py:92
  72.4 8.0 %pad_maximum_fusion = f32[3072,768]{1,0:T(8,128)} fusion(f32[768,768]{1,0:T(8,128)} %convolution_bitcast_fusion, f32[2304,768]{1,0:T(8,128)} %fusion.51), kind=kLoop, calls=%fused_computation.7 | loop fusion | flops 2359296 | bytes 18874368 | tf_op jit(solution)/shard_map/concatenate | solution.py:90
  80.3 2.7 %fusion.21 = bf16[256,768]{1,0:T(8,128)(2,1)} fusion(bf16[256,768]{0,1:T(8,128)(2,1)} %bitcast.116, bf16[768,768]{1,0:T(8,128)(2,1)} %param.21, bf16[256,768]{1,0:T(8,128)(2,1)} %gather_fusion.1, pred[256]{0:T(512)(128)(4,1)S(1)} %compare_and_fusion.1), kind=kOutput, calls=%fused_computation.47 | convolution fusion | flops 302776320 | bytes 2359552 | tf_op jit(solution)/shard_map/dot_general | solution.py:60
  83.1 2.8 %scatter_custom_fusion.1 = bf16[280,768]{1,0:T(8,128)(2,1)} fusion(s32[256]{0:T(256)S(1)} %bitcast.123, bf16[256,768]{1,0:T(8,128)(2,1)} %fusion.21, bf16[]{:T(256)} %constant.20.clone.1), kind=kCustom, calls=%fused_computation.86 | custom fusion | bytes 430592 | tf_op jit(solution)/shard_map/scatter | solution.py:141
  85.9 1.9 reshape.244
  87.8 4.1 %all-to-all-start.1 = ((bf16[8,35,768]{2,1,0:T(8,128)(2,1)}), bf16[8,35,768]{2,1,0:T(8,128)(2,1)}, u32[]{:S(2)}, u32[]{:S(2)}) async-start(bf16[8,35,768]{2,1,0:T(8,128)(2,1)} %reshape.244), calls=%async_computation.2 | async-start | bytes 983040 | tf_op jit(solution)/shard_map/all_to_all | solution.py:143
  92.0 2.3 scatter_custom_fusion
  94.3 1.9 slice_reduce_fusion.48
  96.2 1.9 slice_reduce_fusion.47
  98.1 7.4 %all-to-all-done.1 = bf16[8,35,768]{2,1,0:T(8,128)(2,1)} async-done(((bf16[8,35,768]{2,1,0:T(8,128)(2,1)}), bf16[8,35,768]{2,1,0:T(8,128)(2,1)}, u32[]{:S(2)}, u32[]{:S(2)}) %all-to-all-start.1) | async-done | bytes 430112 | tf_op jit(solution)/shard_map/all_to_all | solution.py:143
  105.5 2.0 reshape.245
  107.5 2.3 %convolution_convert_fusion.3 = bf16[280,384]{1,0:T(8,128)(2,1)} fusion(bf16[280,768]{1,0:T(8,128)(2,1)} %reshape.245, bf16[768,384]{1,0:T(8,128)(2,1)} %param.22), kind=kOutput, calls=%fused_computation.56 | convolution fusion | flops 165258240 | bytes 1234944 | tf_op jit(solution)/shard_map/dot_general | solution.py:151
  109.8 2.9 %scatter_custom_fusion.2 = bf16[1024,384]{1,0:T(8,128)(2,1)} fusion(s32[280]{0:T(512)} %get-tuple-element.53, bf16[280,384]{1,0:T(8,128)(2,1)} %convolution_convert_fusion.3, bf16[]{:T(256)} %constant.20.clone.1), kind=kCustom, calls=%fused_computation.83 | custom fusion | bytes 786944 | tf_op jit(solution)/shard_map/scatter | solution.py:153
  112.8 1.4 broadcast_select_fusion
  114.2 0.6 collective-permute-start.1
  114.8 1.5 collective-permute-start
  116.3 1.0 slice_reduce_fusion.46
  117.2 1.4 collective-permute-done.1
  118.6 0.8 collective-permute-done
  119.7 0.1 pad_maximum_fusion.4
  119.9 3.8 %collective-permute-start.3 = (bf16[38,3,384]{2,1,0:T(4,128)(2,1)S(1)}, bf16[38,3,384]{2,1,0:T(4,128)(2,1)S(1)}, u32[]{:S(2)}, u32[]{:S(2)}) collective-permute-start(bf16[38,3,384]{2,1,0:T(4,128)(2,1)S(1)} %get-tuple-element.58), channel_id=1, source_target_pairs={{4,0},{8,4},{12,8},{0,12},{5,1},{9,5},{13,9},{1,13},{6,2},{10,6},{... | collective-permute-start | bytes 262664 | tf_op jit(solution)/shard_map/ppermute | solution.py:20
  123.7 2.8 %collective-permute-done.2 = bf16[38,3,384]{2,1,0:T(4,128)(2,1)S(1)} collective-permute-done((bf16[38,3,384]{2,1,0:T(4,128)(2,1)S(1)}, bf16[38,3,384]{2,1,0:T(4,128)(2,1)S(1)}, u32[]{:S(2)}, u32[]{:S(2)}) %collective-permute-start.2) | collective-permute-done | bytes 87584 | tf_op jit(solution)/shard_map/ppermute | solution.py:17
  126.5 0.5 maximum_select_fusion
  127.3 11.6 %fusion.66 = (f32[32,32]{1,0:T(8,128)S(1)}, f32[32,32,384]{2,1,0:T(8,128)S(1)}) fusion(bf16[38,38,384]{2,1,0:T(8,128)(2,1)S(1)} %maximum_select_fusion, f32[384]{0:T(512)S(1)} %get-tuple-element.51, f32[384]{0:T(512)S(1)} %get-tuple-element.52, f32[384]{0:T(512)S(1)} %get-tuple-element.5, f32[384]{0:T(512)S(1)} %get-tuple-element.6, ...), kind=kLoop, calls=%fused_computation.165 | loop fusion | flops 57801728 | bytes 40187392 | tf_op jit(solution)/shard_map/reduce_sum | solution.py:26
  138.9 0.4 multiply_reduce_fusion.1
  139.3 0.4 multiply_convert_fusion
  139.7 0.7 copy-done.43
  140.4 8.7 %fusion.4 = bf16[1024,768]{1,0:T(8,128)(2,1)} fusion(bf16[1024,384]{1,0:T(8,128)(2,1)S(1)} %bitcast.114, bf16[384,768]{1,0:T(8,128)(2,1)S(1)} %copy-done.43), kind=kOutput, calls=%fused_computation.11 | convolution fusion | flops 655097856 | bytes 2949120 | tf_op jit(solution)/shard_map/dot_general | solution.py:178
  149.1 3.8 %fusion.20 = f32[1024,128]{1,0:T(8,128)} fusion(bf16[384,128]{1,0:T(8,128)(2,1)} %param.27, bf16[1024,384]{1,0:T(8,128)(2,1)} %copy-done.2, bf16[1024,768]{1,0:T(8,128)(2,1)} %fusion.4, bf16[768,384]{1,0:T(8,128)(2,1)} %param.26), kind=kOutput, calls=%fused_computation.46 | convolution fusion | flops 705822720 | bytes 3571712 | tf_op jit(solution)/shard_map/dot_general | solution.py:184
  152.9 60.6 %reduce-scatter.2.cloned.1.call-done = f32[96,768]{1,0:T(8,128)} async-done(((f32[3072,768]{1,0:T(8,128)}), f32[96,768]{1,0:T(8,128)}) %reduce-scatter.2.cloned.1.call-update) | async-done | bytes 294928 | tf_op jit(solution)/shard_map/reduce_scatter | solution.py:136
  213.5 1.0 convert_element_type.212
  214.4 7.2 %all_gather.3 = bf16[384,768]{1,0:T(8,128)(2,1)S(1)} all-gather(bf16[96,768]{1,0:T(8,128)(2,1)S(1)} %convert_element_type.212), channel_id=1, replica_groups=mesh['eta'=2,'phi'=4,'replica'=4] {'replica'}, dimensions={0}, use_global_device_ids=true | all-gather | bytes 737280 | tf_op jit(solution)/shard_map/all_gather | solution.py:137
  221.7 1.1 convert_element_type.213
  (101 shorter events, 0.4 us)
Async XLA Ops:
  7.2 40.5 %copy-start = (bf16[768,2304]{1,0:T(8,128)(2,1)S(1)}, bf16[768,2304]{1,0:T(8,128)(2,1)}, u32[]{:S(2)}) copy-start(bf16[768,2304]{1,0:T(8,128)(2,1)} %param.19) | copy-start | bytes 10616836
  18.0 22.0 %all-to-all-start = ((bf16[8,35,768]{2,1,0:T(8,128)(2,1)}), bf16[8,35,768]{2,1,0:T(8,128)(2,1)}, u32[]{:S(2)}, u32[]{:S(2)}) async-start(bf16[8,35,768]{2,1,0:T(8,128)(2,1)} %broadcast_select_fusion.1), calls=%async_computation | async-start | bytes 983040 | tf_op jit(solution)/shard_map/all_to_all | solution.py:129
  25.3 4.6 %copy-start.42 = (s32[1,1,1,256]{3,2,1,0:T(1,128)S(1)}, s32[1,1,1,256]{3,2,1,0:T(1,128)}, u32[]{:S(2)}) copy-start(s32[1,1,1,256]{3,2,1,0:T(1,128)} %param.16) | copy-start | bytes 3076
  25.3 5.3 %copy-start.41 = (s32[1,1,1,256]{3,2,1,0:T(1,128)S(1)}, s32[1,1,1,256]{3,2,1,0:T(1,128)}, u32[]{:S(2)}) copy-start(s32[1,1,1,256]{3,2,1,0:T(1,128)} %param.17) | copy-start | bytes 3076
  25.3 188.2 %reduce-scatter.2.cloned.1.call-start = ((), (), s32[]{:S(2)}) async-start(), calls=%async_computation.3 | async-start | bytes 9732096 | tf_op jit(solution)/shard_map/reduce_scatter | solution.py:136
  50.3 0.8 copy-start.6
  50.4 0.8 copy-start.44
  54.6 1.0 copy-start.5
  55.4 9.4 %copy-start.4 = (bf16[12,64,256]{2,1,0:T(8,128)(2,1)}, bf16[12,64,256]{2,1,0:T(8,128)(2,1)S(1)}, u32[]{:S(2)}) copy-start(bf16[12,64,256]{2,1,0:T(8,128)(2,1)S(1)} %convolution_convert_fusion) | copy-start | bytes 1179652
  61.7 3.1 %copy-start.3 = (bf16[1,1,1,256,768]{4,3,2,1,0:T(8,128)(2,1)S(1)}, bf16[1,1,1,256,768]{4,3,2,1,0:T(8,128)(2,1)}, u32[]{:S(2)}) copy-start(bf16[1,1,1,256,768]{4,3,2,1,0:T(8,128)(2,1)} %param.18) | copy-start | bytes 1179652
  67.3 1.0 copy-start.1
  87.8 17.7 %all-to-all-start.1 = ((bf16[8,35,768]{2,1,0:T(8,128)(2,1)}), bf16[8,35,768]{2,1,0:T(8,128)(2,1)}, u32[]{:S(2)}, u32[]{:S(2)}) async-start(bf16[8,35,768]{2,1,0:T(8,128)(2,1)} %reshape.244), calls=%async_computation.2 | async-start | bytes 983040 | tf_op jit(solution)/shard_map/all_to_all | solution.py:143
  114.2 12.8 %copy-start.2 = (bf16[1024,384]{1,0:T(8,128)(2,1)}, bf16[1024,384]{1,0:T(8,128)(2,1)S(1)}, u32[]{:S(2)}) copy-start(bf16[1024,384]{1,0:T(8,128)(2,1)S(1)} %broadcast_select_fusion) | copy-start | bytes 2359300
  114.2 4.4 %collective-permute-start.1 = (bf16[3,32,384]{2,1,0:T(8,128)(2,1)S(1)}, bf16[3,32,384]{2,1,0:T(8,128)(2,1)S(1)}, u32[]{:S(2)}, u32[]{:S(2)}) collective-permute-start(bf16[3,32,384]{2,1,0:T(8,128)(2,1)S(1)} %bitcast.120), channel_id=1, source_target_pairs={{16,0},{0,16},{17,1},{1,17},{18,2},{2,18},{19,3},{3,19},{20,4},{4,... | collective-permute-start | bytes 221192 | tf_op jit(solution)/shard_map/ppermute | solution.py:20
  114.8 4.6 %collective-permute-start = (bf16[3,32,384]{2,1,0:T(8,128)(2,1)S(1)}, bf16[3,32,384]{2,1,0:T(8,128)(2,1)S(1)}, u32[]{:S(2)}, u32[]{:S(2)}) collective-permute-start(bf16[3,32,384]{2,1,0:T(8,128)(2,1)S(1)} %bitcast.119), channel_id=1, source_target_pairs={{0,16},{16,0},{1,17},{17,1},{2,18},{18,2},{3,19},{19,3},{4,20},{20... | collective-permute-start | bytes 221192 | tf_op jit(solution)/shard_map/ppermute | solution.py:17
  119.4 7.6 %copy-start.7 = (f32[384]{0:T(512)S(1)}, f32[384]{0:T(512)}, u32[]{:S(2)}) copy-start(f32[384]{0:T(512)} %get-tuple-element.8) | copy-start | bytes 4612
  119.4 7.6 %copy-start.8 = (f32[384]{0:T(512)S(1)}, f32[384]{0:T(512)}, u32[]{:S(2)}) copy-start(f32[384]{0:T(512)} %get-tuple-element.9) | copy-start | bytes 4612
  119.4 7.6 %copy-start.9 = (f32[384]{0:T(512)S(1)}, f32[384]{0:T(512)}, u32[]{:S(2)}) copy-start(f32[384]{0:T(512)} %get-tuple-element.10) | copy-start | bytes 4612
  119.4 7.6 %copy-start.10 = (f32[384]{0:T(512)S(1)}, f32[384]{0:T(512)}, u32[]{:S(2)}) copy-start(f32[384]{0:T(512)} %get-tuple-element.11) | copy-start | bytes 4612
  119.4 7.6 %copy-start.11 = (f32[384]{0:T(512)S(1)}, f32[384]{0:T(512)}, u32[]{:S(2)}) copy-start(f32[384]{0:T(512)} %get-tuple-element.12) | copy-start | bytes 4612
  119.4 7.6 %copy-start.12 = (f32[384]{0:T(512)S(1)}, f32[384]{0:T(512)}, u32[]{:S(2)}) copy-start(f32[384]{0:T(512)} %get-tuple-element.13) | copy-start | bytes 4612
  119.4 7.6 %copy-start.13 = (f32[384]{0:T(512)S(1)}, f32[384]{0:T(512)}, u32[]{:S(2)}) copy-start(f32[384]{0:T(512)} %get-tuple-element.14) | copy-start | bytes 4612
  119.4 7.6 %copy-start.14 = (f32[384]{0:T(512)S(1)}, f32[384]{0:T(512)}, u32[]{:S(2)}) copy-start(f32[384]{0:T(512)} %get-tuple-element.15) | copy-start | bytes 4612
  119.5 7.6 %copy-start.15 = (f32[384]{0:T(512)S(1)}, f32[384]{0:T(512)}, u32[]{:S(2)}) copy-start(f32[384]{0:T(512)} %get-tuple-element.16) | copy-start | bytes 4612
  119.5 7.6 %copy-start.16 = (f32[384]{0:T(512)S(1)}, f32[384]{0:T(512)}, u32[]{:S(2)}) copy-start(f32[384]{0:T(512)} %get-tuple-element.17) | copy-start | bytes 4612
  119.5 7.6 %copy-start.17 = (f32[384]{0:T(512)S(1)}, f32[384]{0:T(512)}, u32[]{:S(2)}) copy-start(f32[384]{0:T(512)} %get-tuple-element.18) | copy-start | bytes 4612
  119.5 7.6 %copy-start.18 = (f32[384]{0:T(512)S(1)}, f32[384]{0:T(512)}, u32[]{:S(2)}) copy-start(f32[384]{0:T(512)} %get-tuple-element.19) | copy-start | bytes 4612
  119.5 7.6 %copy-start.19 = (f32[384]{0:T(512)S(1)}, f32[384]{0:T(512)}, u32[]{:S(2)}) copy-start(f32[384]{0:T(512)} %get-tuple-element.20) | copy-start | bytes 4612
  119.5 7.6 %copy-start.20 = (f32[384]{0:T(512)S(1)}, f32[384]{0:T(512)}, u32[]{:S(2)}) copy-start(f32[384]{0:T(512)} %get-tuple-element.21) | copy-start | bytes 4612
  119.5 7.6 %copy-start.21 = (f32[384]{0:T(512)S(1)}, f32[384]{0:T(512)}, u32[]{:S(2)}) copy-start(f32[384]{0:T(512)} %get-tuple-element.22) | copy-start | bytes 4612
  119.5 7.6 %copy-start.22 = (f32[384]{0:T(512)S(1)}, f32[384]{0:T(512)}, u32[]{:S(2)}) copy-start(f32[384]{0:T(512)} %get-tuple-element.23) | copy-start | bytes 4612
  119.5 7.6 %copy-start.23 = (f32[384]{0:T(512)S(1)}, f32[384]{0:T(512)}, u32[]{:S(2)}) copy-start(f32[384]{0:T(512)} %get-tuple-element.24) | copy-start | bytes 4612
  119.5 7.6 %copy-start.24 = (f32[384]{0:T(512)S(1)}, f32[384]{0:T(512)}, u32[]{:S(2)}) copy-start(f32[384]{0:T(512)} %get-tuple-element.25) | copy-start | bytes 4612
  119.6 7.6 %copy-start.25 = (f32[384]{0:T(512)S(1)}, f32[384]{0:T(512)}, u32[]{:S(2)}) copy-start(f32[384]{0:T(512)} %get-tuple-element.26) | copy-start | bytes 4612
  119.6 7.6 %copy-start.26 = (f32[384]{0:T(512)S(1)}, f32[384]{0:T(512)}, u32[]{:S(2)}) copy-start(f32[384]{0:T(512)} %get-tuple-element.27) | copy-start | bytes 4612
  119.6 7.6 %copy-start.27 = (f32[384]{0:T(512)S(1)}, f32[384]{0:T(512)}, u32[]{:S(2)}) copy-start(f32[384]{0:T(512)} %get-tuple-element.28) | copy-start | bytes 4612
  119.6 7.6 %copy-start.28 = (f32[384]{0:T(512)S(1)}, f32[384]{0:T(512)}, u32[]{:S(2)}) copy-start(f32[384]{0:T(512)} %get-tuple-element.29) | copy-start | bytes 4612
  119.6 7.6 %copy-start.29 = (f32[384]{0:T(512)S(1)}, f32[384]{0:T(512)}, u32[]{:S(2)}) copy-start(f32[384]{0:T(512)} %get-tuple-element.30) | copy-start | bytes 4612
  119.6 7.6 %copy-start.30 = (f32[384]{0:T(512)S(1)}, f32[384]{0:T(512)}, u32[]{:S(2)}) copy-start(f32[384]{0:T(512)} %get-tuple-element.31) | copy-start | bytes 4612
  119.6 7.6 %copy-start.31 = (f32[384]{0:T(512)S(1)}, f32[384]{0:T(512)}, u32[]{:S(2)}) copy-start(f32[384]{0:T(512)} %get-tuple-element.32) | copy-start | bytes 4612
  119.6 7.6 %copy-start.32 = (f32[384]{0:T(512)S(1)}, f32[384]{0:T(512)}, u32[]{:S(2)}) copy-start(f32[384]{0:T(512)} %get-tuple-element.33) | copy-start | bytes 4612
  119.6 7.6 %copy-start.33 = (f32[384]{0:T(512)S(1)}, f32[384]{0:T(512)}, u32[]{:S(2)}) copy-start(f32[384]{0:T(512)} %get-tuple-element.34) | copy-start | bytes 4612
  119.6 7.6 %copy-start.34 = (f32[384]{0:T(512)S(1)}, f32[384]{0:T(512)}, u32[]{:S(2)}) copy-start(f32[384]{0:T(512)} %get-tuple-element.35) | copy-start | bytes 4612
  119.7 7.6 %copy-start.35 = (f32[384]{0:T(512)S(1)}, f32[384]{0:T(512)}, u32[]{:S(2)}) copy-start(f32[384]{0:T(512)} %get-tuple-element.36) | copy-start | bytes 4612
  119.7 7.6 %copy-start.36 = (f32[384]{0:T(512)S(1)}, f32[384]{0:T(512)}, u32[]{:S(2)}) copy-start(f32[384]{0:T(512)} %get-tuple-element.37) | copy-start | bytes 4612
  119.7 7.6 %copy-start.37 = (f32[384]{0:T(512)S(1)}, f32[384]{0:T(512)}, u32[]{:S(2)}) copy-start(f32[384]{0:T(512)} %get-tuple-element.38) | copy-start | bytes 4612
  119.7 7.6 %copy-start.38 = (f32[384]{0:T(512)S(1)}, f32[384]{0:T(512)}, u32[]{:S(2)}) copy-start(f32[384]{0:T(512)} %get-tuple-element.39) | copy-start | bytes 4612
  119.7 7.6 %copy-start.39 = (f32[384]{0:T(512)S(1)}, f32[384]{0:T(512)}, u32[]{:S(2)}) copy-start(f32[384]{0:T(512)} %get-tuple-element.40) | copy-start | bytes 4612
  119.7 7.6 %copy-start.40 = (f32[384]{0:T(512)S(1)}, f32[384]{0:T(512)}, u32[]{:S(2)}) copy-start(f32[384]{0:T(512)} %get-tuple-element.41) | copy-start | bytes 4612
  119.8 6.7 %collective-permute-start.2 = (bf16[38,3,384]{2,1,0:T(4,128)(2,1)S(1)}, bf16[38,3,384]{2,1,0:T(4,128)(2,1)S(1)}, u32[]{:S(2)}, u32[]{:S(2)}) collective-permute-start(bf16[38,3,384]{2,1,0:T(4,128)(2,1)S(1)} %get-tuple-element.57), channel_id=1, source_target_pairs={{0,4},{4,8},{8,12},{12,0},{1,5},{5,9},{9,13},{13,1},{2,6},{6,10},{... | collective-permute-start | bytes 262664 | tf_op jit(solution)/shard_map/ppermute | solution.py:17
  119.9 6.6 %collective-permute-start.3 = (bf16[38,3,384]{2,1,0:T(4,128)(2,1)S(1)}, bf16[38,3,384]{2,1,0:T(4,128)(2,1)S(1)}, u32[]{:S(2)}, u32[]{:S(2)}) collective-permute-start(bf16[38,3,384]{2,1,0:T(4,128)(2,1)S(1)} %get-tuple-element.58), channel_id=1, source_target_pairs={{4,0},{8,4},{12,8},{0,12},{5,1},{9,5},{13,9},{1,13},{6,2},{10,6},{... | collective-permute-start | bytes 262664 | tf_op jit(solution)/shard_map/ppermute | solution.py:20
  139.3 1.1 copy-start.43
Sparse Core Ops, SparseCore 0:
  80.5 132.9 reduce-scatter.1
where the time goes:
time: 231 us; the launch traced here: 230 us
  waiting for transfers between devices  81.7 us (35%)
  matrix products  42.4 us (18%)
  local copies, waits for them, and re-layouts  33.7 us (15%)
  other arithmetic  32.4 us (14%)
  starting transfers between devices  17.4 us (8%)
  between operations  14.8 us (6%)
  blocking collectives  7.22 us (3%)
    reduce_scatter x1, waiting for transfers between devices, body(): lax.psum_scatter(term, ('eta', 'phi', 'replica'), scatter_dimension=0, ti...  60.6 us
    reduce_sum x2, other arithmetic, plain_norm(): centre = jnp.mean(values, axis=-1, keepdims=True)  12.8 us
    dot_general x1, matrix products, body(): jnp.dot(dec_normed, w_up, preferred_element_type=jnp.float32)  8.74 us
    all_to_all x1, waiting for transfers between devices, body(): lax.all_to_all(outgoing, ('eta', 'phi'), split_axis=0, concat_axis=0, til...  8.72 us
    concatenate x1, other arithmetic, encoder_pass(): jnp.concatenate([lax.dot_general(grad_qkv, normed, contract_rows, preferr...  7.96 us
    all_to_all x1, waiting for transfers between devices, body(): lax.all_to_all(outbound.reshape(group_size, slot_count, feature_width), (...  7.45 us
    all_to_all x1, starting transfers between devices, body(): lax.all_to_all(outgoing, ('eta', 'phi'), split_axis=0, concat_axis=0, til...  7.25 us
    all_gather x1, blocking collectives, body(): lax.all_gather(grad_share.astype(jnp.bfloat16), 'replica', axis=0, tiled=...  7.22 us
  transfers between devices with their start and end apart: 7, of which 6 were waited for; matrix products, arithmetic and copies ran while one was open for 24% of the time, Pallas kernels for 0%

commit v1 on v0

--- a/solution.py
+++ b/solution.py
@@ -6,6 +6,18 @@
 norm_eps = 1e-05
 length_eps = 1e-06
 highest = lax.Precision.HIGHEST
+
+
+def doubled_up(array, axis, dim):
+    ways, here = (lax.axis_size(axis), lax.axis_index(axis))
+    grown, reach = (array, 1)
+    while reach < ways:
+        theirs = lax.ppermute(grown, axis, [(d, d ^ reach) for d in range(ways)])
+        mine_first = jnp.concatenate([grown, theirs], axis=dim)
+        theirs_first = jnp.concatenate([theirs, grown], axis=dim)
+        grown = jnp.where(here & reach == 0, mine_first, theirs_first)
+        reach = 2 * reach
+    return grown
 
 
 def extended(block, sides, width):
@@ -134,9 +146,7 @@
         enc_in, window_id.reshape(-1), enc_cot.reshape(-1, feature_width), w_qkv, head_scale, w_out
     )
     grad_share = lax.psum_scatter(term, ("eta", "phi", "replica"), scatter_dimension=0, tiled=True)
-    grad_total = lax.all_gather(
-        grad_share.astype(jnp.bfloat16), "replica", axis=0, tiled=True
-    ).astype(grad_share.dtype)
+    grad_total = doubled_up(grad_share.astype(jnp.bfloat16), "replica", 0).astype(grad_share.dtype)
     outbound = (
         jnp.zeros((group_size * slot_count, feature_width), jnp.bfloat16).at[sources].set(enc_out)
     )

time: 231 us -> 245 us (1.061)
  waiting for transfers between devices: 81.7 us -> 98.4 us
  blocking collectives: 7.22 us -> 0 us
  other arithmetic: 32.4 us -> 35.3 us
    reduce_scatter x1, waiting for transfers between devices: 60.6 us -> 72.8 us  [body(): lax.psum_scatter(term, ('eta', 'phi', 'replica'), scatter_dimension=0, ti...]
    all_gather x1 -> x0, blocking collectives: 7.22 us -> none  [body(): lax.all_gather(grad_share.astype(jnp.bfloat16), 'replica', axis=0, tiled=...]
    ppermute x0 -> x2, waiting for transfers between devices: none -> 4.45 us  [doubled_up(): theirs = lax.ppermute(grown, axis, [(d, d ^ reach) for d in range(ways)])]
  transfers between devices with their start and end apart: 7 -> 9, of which waited for: 6 -> 7; matrix products, arithmetic and copies ran while one was open for 24% -> 23% of each run, Pallas kernels for 0% -> 0%
where the time goes in v1:
time: 245 us; the launch traced here: 243 us
  waiting for transfers between devices  98.4 us (40%)
  matrix products  42.9 us (18%)
  other arithmetic  35.3 us (14%)
  local copies, waits for them, and re-layouts  32.9 us (13%)
  starting transfers between devices  18.9 us (8%)
  between operations  14.8 us (6%)
    reduce_scatter x1, waiting for transfers between devices, body(): lax.psum_scatter(term, ('eta', 'phi', 'replica'), scatter_dimension=0, ti...  72.8 us
    reduce_sum x2, other arithmetic, plain_norm(): centre = jnp.mean(values, axis=-1, keepdims=True)  12.8 us
    dot_general x1, matrix products, body(): jnp.dot(dec_normed, w_up, preferred_element_type=jnp.float32)  9.25 us
    all_to_all x1, waiting for transfers between devices, body(): lax.all_to_all(outgoing, ('eta', 'phi'), split_axis=0, concat_axis=0, til...  8.72 us
    concatenate x1, other arithmetic, encoder_pass(): jnp.concatenate([lax.dot_general(grad_qkv, normed, contract_rows, preferr...  7.96 us
    all_to_all x1, waiting for transfers between devices, body(): lax.all_to_all(outbound.reshape(group_size, slot_count, feature_width), (...  7.47 us
    all_to_all x1, starting transfers between devices, body(): lax.all_to_all(outgoing, ('eta', 'phi'), split_axis=0, concat_axis=0, til...  7.25 us
    gather x2, local copies, waits for them, and re-layouts, body(): jnp.take(flat_tile, jnp.minimum(slot_cells, tile_len - 1), axis=0)  6.49 us
  transfers between devices with their start and end apart: 9, of which 7 were waited for; matrix products, arithmetic and copies ran while one was open for 23% of the time, Pallas kernels for 0%

profile of v1, /device:TPU:0, one launch (start us, length us, event | category | flops | bytes accessed | tf_op | source)
XLA Modules:
  0.0 243.3 jit_solution(9482490867880476412)
XLA Ops:
  7.2 0.9 reshape.238
  8.1 0.9 compare_and_fusion
  8.9 0.6 fusion.51
  9.5 4.6 %gather_fusion = bf16[280,768]{1,0:T(8,128)(2,1)} fusion(bf16[1024,768]{1,0:T(8,128)(2,1)} %bitcast.102, s32[1024]{0:T(1024)S(1)} %pad_clamp_fusion.1), kind=kCustom, calls=%fused_computation | custom fusion | bytes 861280 | tf_op jit(solution)/shard_map/jit(_take)/gather | solution.py:139
  14.1 1.9 gather.11
  16.0 1.9 broadcast_select_fusion.1
  18.0 7.3 %all-to-all-start = ((bf16[8,35,768]{2,1,0:T(8,128)(2,1)}), bf16[8,35,768]{2,1,0:T(8,128)(2,1)}, u32[]{:S(2)}, u32[]{:S(2)}) async-start(bf16[8,35,768]{2,1,0:T(8,128)(2,1)} %broadcast_select_fusion.1), calls=%async_computation | async-start | bytes 983040 | tf_op jit(solution)/shard_map/all_to_all | solution.py:141
  25.3 2.7 %convolution_convert_fusion.2 = bf16[256,768]{1,0:T(8,128)(2,1)} fusion(bf16[768,768]{1,0:T(8,128)(2,1)} %param.21, bf16[1,1,1,256,768]{4,3,2,1,0:T(8,128)(2,1)} %param.18), kind=kOutput, calls=%fused_computation.52 | convolution fusion | flops 302186496 | bytes 1966080 | tf_op jit(solution)/shard_map/dot_general | solution.py:74
  27.9 1.9 copy.32
  29.9 0.7 compare_and_fusion.1
  30.6 0.7 broadcast_compare_fusion
  31.3 8.7 %all-to-all-done = bf16[8,35,768]{2,1,0:T(8,128)(2,1)} async-done(((bf16[8,35,768]{2,1,0:T(8,128)(2,1)}), bf16[8,35,768]{2,1,0:T(8,128)(2,1)}, u32[]{:S(2)}, u32[]{:S(2)}) %all-to-all-start) | async-done | bytes 430112 | tf_op jit(solution)/shard_map/all_to_all | solution.py:141
  40.0 1.9 reshape.239
  41.9 3.2 %gather_fusion.1 = bf16[256,768]{1,0:T(8,128)(2,1)} fusion(bf16[280,768]{1,0:T(8,128)(2,1)} %reshape.239, s32[1024]{0:T(1024)S(1)} %pad_clamp_fusion), kind=kCustom, calls=%fused_computation.1 | custom fusion | bytes 787456 | tf_op jit(solution)/shard_map/jit(_take)/gather | solution.py:144
  45.1 1.2 convert_reduce_fusion
  46.4 1.3 fusion.29
  47.7 2.6 %fusion.54 = f32[256,2304]{0,1:T(8,128)S(1)} fusion(bf16[768,2304]{1,0:T(8,128)(2,1)S(1)} %copy-done, f32[256]{0:T(256)S(1)} %add_rsqrt_fusion.1, f32[256]{0:T(256)S(1)} %broadcast_multiply_fusion.1, bf16[256,768]{1,0:T(8,128)(2,1)} %gather_fusion.1, pred[256]{0:T(512)(128)(4,1)S(1)} %compare_and_fusion.1), kind=kOutput, calls=%fused_computation.166 | convolution fusion | flops 906952704 | bytes 6293760 | tf_op jit(solution)/shard_map/dot_general | solution.py:49
  50.3 0.2 multiply_reduce_fusion.3
  50.5 0.6 copy-done.6
  51.2 3.4 %fusion.13 = (f32[12,256]{1,0:T(8,128)S(1)}, f32[12,256,256]{1,2,0:T(8,128)S(1)}) fusion(f32[12]{0:T(128)S(1)} %copy-done.43, pred[256,256]{0,1:T(8,128)(4,1)S(1)} %copy-done.6, f32[256,3,12,64]{0,3,2,1:T(8,128)S(1)} %bitcast.104, f32[256,12]{0,1:T(8,128)S(1)} %get-tuple-element.66, f32[256,12]{0,1:T(8,128)S(1)} %get-tuple-element.65), kind=kOutput, calls=%fused_computation.31 | convolution fusion | flops 606729216 | bytes 4829696 | tf_op jit(solution)/shard_map/qhd,khd->hqk/dot_general | solution.py:61
  54.5 0.9 convolution_convert_fusion
  55.4 0.1 copy-done.5
  55.5 1.2 multiply_reduce_fusion
  56.7 3.3 %convolution_bitcast_fusion.2 = f32[256,12,64]{0,2,1:T(8,128)S(1)} fusion(f32[12,256,256]{1,2,0:T(8,128)S(1)} %get-tuple-element.64, f32[12,256]{1,0:T(8,128)S(1)} %get-tuple-element.63, f32[12]{0:T(128)S(1)} %copy-done.43, f32[256,3,12,64]{0,3,2,1:T(8,128)S(1)} %bitcast.107, f32[256,12]{0,1:T(8,128)S(1)} %get-tuple-element.66, ...), kind=kOutput, calls=%fused_computation.45 | convolution fusion | flops 608894976 | bytes 7979520 | tf_op jit(solution)/shard_map/hqk,khd->qhd/dot_general | solution.py:88
  60.0 4.0 %convolution_bitcast_fusion.1 = f32[256,12,64]{0,2,1:T(8,128)S(1)} fusion(f32[12,256,256]{1,2,0:T(8,128)S(1)} %get-tuple-element.64, f32[12,256]{1,0:T(8,128)S(1)} %get-tuple-element.63, f32[12]{0:T(128)S(1)} %copy-done.43, f32[256,3,12,64]{0,3,2,1:T(8,128)S(1)} %bitcast.108, f32[256,12]{0,1:T(8,128)S(1)} %get-tuple-element.65, ...), kind=kOutput, calls=%fused_computation.44 | convolution fusion | flops 608894976 | bytes 7979520 | tf_op jit(solution)/shard_map/hqk,qhd->khd/dot_general | solution.py:89
  63.9 0.9 fusion.24
  64.8 0.2 fusion.26
  65.1 0.2 fusion.25
  65.3 0.1 pad_maximum_fusion.1
  65.5 0.8 copy-done.1
  66.3 4.1 %fusion.52 = f32[2304,768]{1,0:T(8,128)} fusion(bf16[256,2304]{0,1:T(8,128)(2,1)S(1)} %bitcast.101, f32[256]{0:T(256)S(1)} %add_rsqrt_fusion.1, f32[256]{0:T(256)S(1)} %broadcast_multiply_fusion.1, bf16[256,768]{1,0:T(8,128)(2,1)S(1)} %copy-done.1, pred[256]{0:T(512)(128)(4,1)S(1)} %compare_and_fusion.1), kind=kOutput, calls=%fused_computation.165 | convolution fusion | flops 906952704 | bytes 8653056 | tf_op jit(solution)/shard_map/dot_general | solution.py:104
  70.4 1.9 convolution_bitcast_fusion
  72.3 8.0 %pad_maximum_fusion = f32[3072,768]{1,0:T(8,128)} fusion(f32[768,768]{1,0:T(8,128)} %convolution_bitcast_fusion, f32[2304,768]{1,0:T(8,128)} %fusion.52), kind=kLoop, calls=%fused_computation.7 | loop fusion | flops 2359296 | bytes 18874368 | tf_op jit(solution)/shard_map/concatenate | solution.py:102
  80.3 2.7 %fusion.21 = bf16[256,768]{1,0:T(8,128)(2,1)} fusion(bf16[256,768]{0,1:T(8,128)(2,1)} %bitcast.113, bf16[768,768]{1,0:T(8,128)(2,1)} %param.21, bf16[256,768]{1,0:T(8,128)(2,1)} %gather_fusion.1, pred[256]{0:T(512)(128)(4,1)S(1)} %compare_and_fusion.1), kind=kOutput, calls=%fused_computation.47 | convolution fusion | flops 302776320 | bytes 2359552 | tf_op jit(solution)/shard_map/dot_general | solution.py:72
  83.0 2.8 %scatter_custom_fusion.1 = bf16[280,768]{1,0:T(8,128)(2,1)} fusion(s32[256]{0:T(256)S(1)} %bitcast.120, bf16[256,768]{1,0:T(8,128)(2,1)} %fusion.21, bf16[]{:T(256)} %constant.23.clone.1), kind=kCustom, calls=%fused_computation.89 | custom fusion | bytes 430592 | tf_op jit(solution)/shard_map/scatter | solution.py:151
  85.9 1.9 reshape.244
  87.8 4.1 %all-to-all-start.1 = ((bf16[8,35,768]{2,1,0:T(8,128)(2,1)}), bf16[8,35,768]{2,1,0:T(8,128)(2,1)}, u32[]{:S(2)}, u32[]{:S(2)}) async-start(bf16[8,35,768]{2,1,0:T(8,128)(2,1)} %reshape.244), calls=%async_computation.2 | async-start | bytes 983040 | tf_op jit(solution)/shard_map/all_to_all | solution.py:153
  92.0 2.2 scatter_custom_fusion
  94.2 1.9 slice_reduce_fusion.48
  96.1 1.9 slice_reduce_fusion.47
  98.0 7.5 %all-to-all-done.1 = bf16[8,35,768]{2,1,0:T(8,128)(2,1)} async-done(((bf16[8,35,768]{2,1,0:T(8,128)(2,1)}), bf16[8,35,768]{2,1,0:T(8,128)(2,1)}, u32[]{:S(2)}, u32[]{:S(2)}) %all-to-all-start.1) | async-done | bytes 430112 | tf_op jit(solution)/shard_map/all_to_all | solution.py:153
  105.5 2.0 reshape.245
  107.5 2.3 convolution_convert_fusion.3
  109.8 2.9 %scatter_custom_fusion.2 = bf16[1024,384]{1,0:T(8,128)(2,1)} fusion(s32[280]{0:T(512)} %get-tuple-element.53, bf16[280,384]{1,0:T(8,128)(2,1)} %convolution_convert_fusion.3, bf16[]{:T(256)} %constant.23.clone.1), kind=kCustom, calls=%fused_computation.85 | custom fusion | bytes 786944 | tf_op jit(solution)/shard_map/scatter | solution.py:163
  112.7 1.4 broadcast_select_fusion
  114.2 0.6 collective-permute-start.2
  114.8 1.5 collective-permute-start.3
  116.3 1.0 slice_reduce_fusion.46
  117.2 1.4 collective-permute-done.2
  118.6 0.8 collective-permute-done.3
  119.8 3.8 %collective-permute-start.5 = (bf16[38,3,384]{2,1,0:T(4,128)(2,1)S(1)}, bf16[38,3,384]{2,1,0:T(4,128)(2,1)S(1)}, u32[]{:S(2)}, u32[]{:S(2)}) collective-permute-start(bf16[38,3,384]{2,1,0:T(4,128)(2,1)S(1)} %get-tuple-element.58), channel_id=1, source_target_pairs={{4,0},{8,4},{12,8},{0,12},{5,1},{9,5},{13,9},{1,13},{6,2},{10,6},{... | collective-permute-start | bytes 262664 | tf_op jit(solution)/shard_map/ppermute | solution.py:32
  123.7 2.8 %collective-permute-done.4 = bf16[38,3,384]{2,1,0:T(4,128)(2,1)S(1)} collective-permute-done((bf16[38,3,384]{2,1,0:T(4,128)(2,1)S(1)}, bf16[38,3,384]{2,1,0:T(4,128)(2,1)S(1)}, u32[]{:S(2)}, u32[]{:S(2)}) %collective-permute-start.4) | collective-permute-done | bytes 87584 | tf_op jit(solution)/shard_map/ppermute | solution.py:29
  126.5 0.5 maximum_select_fusion
  127.3 11.6 %fusion.67 = (f32[32,32]{1,0:T(8,128)S(1)}, f32[32,32,384]{2,1,0:T(8,128)S(1)}) fusion(bf16[38,38,384]{2,1,0:T(8,128)(2,1)S(1)} %maximum_select_fusion, f32[384]{0:T(512)S(1)} %get-tuple-element.51, f32[384]{0:T(512)S(1)} %get-tuple-element.52, f32[384]{0:T(512)S(1)} %get-tuple-element.5, f32[384]{0:T(512)S(1)} %get-tuple-element.6, ...), kind=kLoop, calls=%fused_computation.168 | loop fusion | flops 57801728 | bytes 40187392 | tf_op jit(solution)/shard_map/reduce_sum | solution.py:38
  138.9 0.4 multiply_reduce_fusion.1
  139.3 1.2 multiply_convert_fusion
  140.5 72.8 %reduce-scatter.2.cloned.1.call-done = f32[96,768]{1,0:T(8,128)} async-done(((f32[3072,768]{1,0:T(8,128)}), f32[96,768]{1,0:T(8,128)}) %reduce-scatter.2.cloned.1.call-update) | async-done | bytes 294928 | tf_op jit(solution)/shard_map/reduce_scatter | solution.py:148
  213.3 1.0 convert_element_type.212
  214.4 9.3 %fusion.4 = bf16[1024,768]{1,0:T(8,128)(2,1)} fusion(bf16[1024,384]{1,0:T(8,128)(2,1)} %bitcast.111, bf16[384,768]{1,0:T(8,128)(2,1)} %param.25), kind=kOutput, calls=%fused_computation.11 | convolution fusion | flops 655097856 | bytes 2949120 | tf_op jit(solution)/shard_map/dot_general | solution.py:188
  223.7 0.8 maximum_select_fusion.2
  224.4 1.5 collective-permute-start.1
  225.9 3.8 %fusion.20 = f32[1024,128]{1,0:T(8,128)} fusion(bf16[384,128]{1,0:T(8,128)(2,1)} %param.27, bf16[1024,384]{1,0:T(8,128)(2,1)} %copy-done.2, bf16[1024,768]{1,0:T(8,128)(2,1)} %fusion.4, bf16[768,384]{1,0:T(8,128)(2,1)} %param.26), kind=kOutput, calls=%fused_computation.46 | convolution fusion | flops 705822720 | bytes 3571712 | tf_op jit(solution)/shard_map/dot_general | solution.py:194
  229.7 4.5 %collective-permute-done.1 = bf16[192,768]{1,0:T(8,128)(2,1)} collective-permute-done((bf16[192,768]{1,0:T(8,128)(2,1)}, bf16[192,768]{1,0:T(8,128)(2,1)}, u32[]{:S(2)}, u32[]{:S(2)}) %collective-permute-start.1) | collective-permute-done | bytes 294944 | tf_op jit(solution)/shard_map/ppermute | solution.py:15
  234.1 2.4 fusion.37
  (103 shorter events, 0.6 us)
Async XLA Ops:
  7.2 40.5 %copy-start = (bf16[768,2304]{1,0:T(8,128)(2,1)S(1)}, bf16[768,2304]{1,0:T(8,128)(2,1)}, u32[]{:S(2)}) copy-start(bf16[768,2304]{1,0:T(8,128)(2,1)} %param.19) | copy-start | bytes 10616836
  18.0 22.0 %all-to-all-start = ((bf16[8,35,768]{2,1,0:T(8,128)(2,1)}), bf16[8,35,768]{2,1,0:T(8,128)(2,1)}, u32[]{:S(2)}, u32[]{:S(2)}) async-start(bf16[8,35,768]{2,1,0:T(8,128)(2,1)} %broadcast_select_fusion.1), calls=%async_computation | async-start | bytes 983040 | tf_op jit(solution)/shard_map/all_to_all | solution.py:141
  25.2 4.6 %copy-start.42 = (s32[1,1,1,256]{3,2,1,0:T(1,128)S(1)}, s32[1,1,1,256]{3,2,1,0:T(1,128)}, u32[]{:S(2)}) copy-start(s32[1,1,1,256]{3,2,1,0:T(1,128)} %param.16) | copy-start | bytes 3076
  25.2 5.3 %copy-start.41 = (s32[1,1,1,256]{3,2,1,0:T(1,128)S(1)}, s32[1,1,1,256]{3,2,1,0:T(1,128)}, u32[]{:S(2)}) copy-start(s32[1,1,1,256]{3,2,1,0:T(1,128)} %param.17) | copy-start | bytes 3076
  25.2 188.1 %reduce-scatter.2.cloned.1.call-start = ((), (), s32[]{:S(2)}) async-start(), calls=%async_computation.3 | async-start | bytes 9732096 | tf_op jit(solution)/shard_map/reduce_scatter | solution.py:148
  50.3 0.8 copy-start.6
  50.3 0.8 copy-start.43
  54.5 1.0 copy-start.5
  55.4 15.0 %copy-start.4 = (bf16[12,64,256]{2,1,0:T(8,128)(2,1)}, bf16[12,64,256]{2,1,0:T(8,128)(2,1)S(1)}, u32[]{:S(2)}) copy-start(bf16[12,64,256]{2,1,0:T(8,128)(2,1)S(1)} %convolution_convert_fusion) | copy-start | bytes 1179652
  65.3 1.0 copy-start.1
  66.3 4.1 %copy-start.3 = (bf16[1,1,1,256,768]{4,3,2,1,0:T(8,128)(2,1)S(1)}, bf16[1,1,1,256,768]{4,3,2,1,0:T(8,128)(2,1)}, u32[]{:S(2)}) copy-start(bf16[1,1,1,256,768]{4,3,2,1,0:T(8,128)(2,1)} %param.18) | copy-start | bytes 1179652
  87.8 17.7 %all-to-all-start.1 = ((bf16[8,35,768]{2,1,0:T(8,128)(2,1)}), bf16[8,35,768]{2,1,0:T(8,128)(2,1)}, u32[]{:S(2)}, u32[]{:S(2)}) async-start(bf16[8,35,768]{2,1,0:T(8,128)(2,1)} %reshape.244), calls=%async_computation.2 | async-start | bytes 983040 | tf_op jit(solution)/shard_map/all_to_all | solution.py:153
  114.1 12.8 %copy-start.2 = (bf16[1024,384]{1,0:T(8,128)(2,1)}, bf16[1024,384]{1,0:T(8,128)(2,1)S(1)}, u32[]{:S(2)}) copy-start(bf16[1024,384]{1,0:T(8,128)(2,1)S(1)} %broadcast_select_fusion) | copy-start | bytes 2359300
  114.2 4.4 %collective-permute-start.2 = (bf16[3,32,384]{2,1,0:T(8,128)(2,1)S(1)}, bf16[3,32,384]{2,1,0:T(8,128)(2,1)S(1)}, u32[]{:S(2)}, u32[]{:S(2)}) collective-permute-start(bf16[3,32,384]{2,1,0:T(8,128)(2,1)S(1)} %bitcast.117), channel_id=1, source_target_pairs={{0,16},{16,0},{1,17},{17,1},{2,18},{18,2},{3,19},{19,3},{4,20},{20... | collective-permute-start | bytes 221192 | tf_op jit(solution)/shard_map/ppermute | solution.py:29
  114.8 4.6 %collective-permute-start.3 = (bf16[3,32,384]{2,1,0:T(8,128)(2,1)S(1)}, bf16[3,32,384]{2,1,0:T(8,128)(2,1)S(1)}, u32[]{:S(2)}, u32[]{:S(2)}) collective-permute-start(bf16[3,32,384]{2,1,0:T(8,128)(2,1)S(1)} %bitcast.116), channel_id=1, source_target_pairs={{16,0},{0,16},{17,1},{1,17},{18,2},{2,18},{19,3},{3,19},{20,4},{4,... | collective-permute-start | bytes 221192 | tf_op jit(solution)/shard_map/ppermute | solution.py:32
  119.4 7.6 %copy-start.7 = (f32[384]{0:T(512)S(1)}, f32[384]{0:T(512)}, u32[]{:S(2)}) copy-start(f32[384]{0:T(512)} %get-tuple-element.8) | copy-start | bytes 4612
  119.4 7.6 %copy-start.8 = (f32[384]{0:T(512)S(1)}, f32[384]{0:T(512)}, u32[]{:S(2)}) copy-start(f32[384]{0:T(512)} %get-tuple-element.9) | copy-start | bytes 4612
  119.4 7.6 %copy-start.9 = (f32[384]{0:T(512)S(1)}, f32[384]{0:T(512)}, u32[]{:S(2)}) copy-start(f32[384]{0:T(512)} %get-tuple-element.10) | copy-start | bytes 4612
  119.4 7.6 %copy-start.10 = (f32[384]{0:T(512)S(1)}, f32[384]{0:T(512)}, u32[]{:S(2)}) copy-start(f32[384]{0:T(512)} %get-tuple-element.11) | copy-start | bytes 4612
  119.4 7.6 %copy-start.11 = (f32[384]{0:T(512)S(1)}, f32[384]{0:T(512)}, u32[]{:S(2)}) copy-start(f32[384]{0:T(512)} %get-tuple-element.12) | copy-start | bytes 4612
  119.4 7.6 %copy-start.12 = (f32[384]{0:T(512)S(1)}, f32[384]{0:T(512)}, u32[]{:S(2)}) copy-start(f32[384]{0:T(512)} %get-tuple-element.13) | copy-start | bytes 4612
  119.4 7.6 %copy-start.13 = (f32[384]{0:T(512)S(1)}, f32[384]{0:T(512)}, u32[]{:S(2)}) copy-start(f32[384]{0:T(512)} %get-tuple-element.14) | copy-start | bytes 4612
  119.4 7.6 %copy-start.14 = (f32[384]{0:T(512)S(1)}, f32[384]{0:T(512)}, u32[]{:S(2)}) copy-start(f32[384]{0:T(512)} %get-tuple-element.15) | copy-start | bytes 4612
  119.4 7.6 %copy-start.15 = (f32[384]{0:T(512)S(1)}, f32[384]{0:T(512)}, u32[]{:S(2)}) copy-start(f32[384]{0:T(512)} %get-tuple-element.16) | copy-start | bytes 4612
  119.4 7.6 %copy-start.16 = (f32[384]{0:T(512)S(1)}, f32[384]{0:T(512)}, u32[]{:S(2)}) copy-start(f32[384]{0:T(512)} %get-tuple-element.17) | copy-start | bytes 4612
  119.4 7.6 %copy-start.17 = (f32[384]{0:T(512)S(1)}, f32[384]{0:T(512)}, u32[]{:S(2)}) copy-start(f32[384]{0:T(512)} %get-tuple-element.18) | copy-start | bytes 4612
  119.5 7.6 %copy-start.18 = (f32[384]{0:T(512)S(1)}, f32[384]{0:T(512)}, u32[]{:S(2)}) copy-start(f32[384]{0:T(512)} %get-tuple-element.19) | copy-start | bytes 4612
  119.5 7.6 %copy-start.19 = (f32[384]{0:T(512)S(1)}, f32[384]{0:T(512)}, u32[]{:S(2)}) copy-start(f32[384]{0:T(512)} %get-tuple-element.20) | copy-start | bytes 4612
  119.5 7.6 %copy-start.20 = (f32[384]{0:T(512)S(1)}, f32[384]{0:T(512)}, u32[]{:S(2)}) copy-start(f32[384]{0:T(512)} %get-tuple-element.21) | copy-start | bytes 4612
  119.5 7.6 %copy-start.21 = (f32[384]{0:T(512)S(1)}, f32[384]{0:T(512)}, u32[]{:S(2)}) copy-start(f32[384]{0:T(512)} %get-tuple-element.22) | copy-start | bytes 4612
  119.5 7.6 %copy-start.22 = (f32[384]{0:T(512)S(1)}, f32[384]{0:T(512)}, u32[]{:S(2)}) copy-start(f32[384]{0:T(512)} %get-tuple-element.23) | copy-start | bytes 4612
  119.5 7.6 %copy-start.23 = (f32[384]{0:T(512)S(1)}, f32[384]{0:T(512)}, u32[]{:S(2)}) copy-start(f32[384]{0:T(512)} %get-tuple-element.24) | copy-start | bytes 4612
  119.5 7.6 %copy-start.24 = (f32[384]{0:T(512)S(1)}, f32[384]{0:T(512)}, u32[]{:S(2)}) copy-start(f32[384]{0:T(512)} %get-tuple-element.25) | copy-start | bytes 4612
  119.5 7.6 %copy-start.25 = (f32[384]{0:T(512)S(1)}, f32[384]{0:T(512)}, u32[]{:S(2)}) copy-start(f32[384]{0:T(512)} %get-tuple-element.26) | copy-start | bytes 4612
  119.5 7.6 %copy-start.26 = (f32[384]{0:T(512)S(1)}, f32[384]{0:T(512)}, u32[]{:S(2)}) copy-start(f32[384]{0:T(512)} %get-tuple-element.27) | copy-start | bytes 4612
  119.5 7.6 %copy-start.27 = (f32[384]{0:T(512)S(1)}, f32[384]{0:T(512)}, u32[]{:S(2)}) copy-start(f32[384]{0:T(512)} %get-tuple-element.28) | copy-start | bytes 4612
  119.5 7.6 %copy-start.28 = (f32[384]{0:T(512)S(1)}, f32[384]{0:T(512)}, u32[]{:S(2)}) copy-start(f32[384]{0:T(512)} %get-tuple-element.29) | copy-start | bytes 4612
  119.6 7.6 %copy-start.29 = (f32[384]{0:T(512)S(1)}, f32[384]{0:T(512)}, u32[]{:S(2)}) copy-start(f32[384]{0:T(512)} %get-tuple-element.30) | copy-start | bytes 4612
  119.6 7.6 %copy-start.30 = (f32[384]{0:T(512)S(1)}, f32[384]{0:T(512)}, u32[]{:S(2)}) copy-start(f32[384]{0:T(512)} %get-tuple-element.31) | copy-start | bytes 4612
  119.6 7.6 %copy-start.31 = (f32[384]{0:T(512)S(1)}, f32[384]{0:T(512)}, u32[]{:S(2)}) copy-start(f32[384]{0:T(512)} %get-tuple-element.32) | copy-start | bytes 4612
  119.6 7.6 %copy-start.32 = (f32[384]{0:T(512)S(1)}, f32[384]{0:T(512)}, u32[]{:S(2)}) copy-start(f32[384]{0:T(512)} %get-tuple-element.33) | copy-start | bytes 4612
  119.6 7.6 %copy-start.33 = (f32[384]{0:T(512)S(1)}, f32[384]{0:T(512)}, u32[]{:S(2)}) copy-start(f32[384]{0:T(512)} %get-tuple-element.34) | copy-start | bytes 4612
  119.6 7.6 %copy-start.34 = (f32[384]{0:T(512)S(1)}, f32[384]{0:T(512)}, u32[]{:S(2)}) copy-start(f32[384]{0:T(512)} %get-tuple-element.35) | copy-start | bytes 4612
  119.6 7.6 %copy-start.35 = (f32[384]{0:T(512)S(1)}, f32[384]{0:T(512)}, u32[]{:S(2)}) copy-start(f32[384]{0:T(512)} %get-tuple-element.36) | copy-start | bytes 4612
  119.6 7.6 %copy-start.36 = (f32[384]{0:T(512)S(1)}, f32[384]{0:T(512)}, u32[]{:S(2)}) copy-start(f32[384]{0:T(512)} %get-tuple-element.37) | copy-start | bytes 4612
  119.6 7.6 %copy-start.37 = (f32[384]{0:T(512)S(1)}, f32[384]{0:T(512)}, u32[]{:S(2)}) copy-start(f32[384]{0:T(512)} %get-tuple-element.38) | copy-start | bytes 4612
  119.7 7.6 %copy-start.38 = (f32[384]{0:T(512)S(1)}, f32[384]{0:T(512)}, u32[]{:S(2)}) copy-start(f32[384]{0:T(512)} %get-tuple-element.39) | copy-start | bytes 4612
  119.7 7.6 %copy-start.39 = (f32[384]{0:T(512)S(1)}, f32[384]{0:T(512)}, u32[]{:S(2)}) copy-start(f32[384]{0:T(512)} %get-tuple-element.40) | copy-start | bytes 4612
  119.7 7.6 %copy-start.40 = (f32[384]{0:T(512)S(1)}, f32[384]{0:T(512)}, u32[]{:S(2)}) copy-start(f32[384]{0:T(512)} %get-tuple-element.41) | copy-start | bytes 4612
  119.8 6.7 %collective-permute-start.4 = (bf16[38,3,384]{2,1,0:T(4,128)(2,1)S(1)}, bf16[38,3,384]{2,1,0:T(4,128)(2,1)S(1)}, u32[]{:S(2)}, u32[]{:S(2)}) collective-permute-start(bf16[38,3,384]{2,1,0:T(4,128)(2,1)S(1)} %get-tuple-element.57), channel_id=1, source_target_pairs={{0,4},{4,8},{8,12},{12,0},{1,5},{5,9},{9,13},{13,1},{2,6},{6,10},{... | collective-permute-start | bytes 262664 | tf_op jit(solution)/shard_map/ppermute | solution.py:29
  119.8 6.6 %collective-permute-start.5 = (bf16[38,3,384]{2,1,0:T(4,128)(2,1)S(1)}, bf16[38,3,384]{2,1,0:T(4,128)(2,1)S(1)}, u32[]{:S(2)}, u32[]{:S(2)}) collective-permute-start(bf16[38,3,384]{2,1,0:T(4,128)(2,1)S(1)} %get-tuple-element.58), channel_id=1, source_target_pairs={{4,0},{8,4},{12,8},{0,12},{5,1},{9,5},{13,9},{1,13},{6,2},{10,6},{... | collective-permute-start | bytes 262664 | tf_op jit(solution)/shard_map/ppermute | solution.py:32
  214.3 9.3 %collective-permute-start = (bf16[96,768]{1,0:T(8,128)(2,1)S(1)}, bf16[96,768]{1,0:T(8,128)(2,1)S(1)}, u32[]{:S(2)}, u32[]{:S(2)}) collective-permute-start(bf16[96,768]{1,0:T(8,128)(2,1)S(1)} %convert_element_type.212), channel_id=1, source_target_pairs={{0,1},{1,0},{2,3},{3,2},{4,5},{5,4},{6,7},{7,6},{8,9},{9,8},{10,11... | collective-permute-start | bytes 442376 | tf_op jit(solution)/shard_map/ppermute | solution.py:15
  224.4 9.7 %collective-permute-start.1 = (bf16[192,768]{1,0:T(8,128)(2,1)}, bf16[192,768]{1,0:T(8,128)(2,1)}, u32[]{:S(2)}, u32[]{:S(2)}) collective-permute-start(bf16[192,768]{1,0:T(8,128)(2,1)} %maximum_select_fusion.2), channel_id=1, source_target_pairs={{0,2},{1,3},{2,0},{3,1},{4,6},{5,7},{6,4},{7,5},{8,10},{9,11},{10,... | collective-permute-start | bytes 884744 | tf_op jit(solution)/shard_map/ppermute | solution.py:15
Sparse Core Ops, SparseCore 0:
  80.4 132.8 reduce-scatter.1
